TPU v7x, 32 devices: a whole 2x2x4 slice. The times are simulated.
32 devices in a mesh: gz: 32 (over z, y, x, core).
Axes of the slice: x: 2, y: 2, z: 4, core: 2. Of those that a mesh axis runs over, the one named last changes fastest.
Arguments:
- marker_positions: float32 [4096, 3, 256], P('gz'), may hold values from 0 to 1
- marker_forces: float32 [4096, 3, 256], P('gz'), may hold values from -48 to 48
- dest_slab: int32 [4096, 1], P('gz'), may hold values from 0 to 31; in each aligned block of 128 rows (0 to 127, 128 to 255, ...) at most 8 rows name the same one
- base_cells: int32 [4096, 2], P('gz'), may hold values from 0 to 127
- fluid_source: float32 [128, 3, 128, 128], P('gz'), may hold values from -7 to 7
Outputs:
- velocity: float32 [128, 3, 128, 128], P('gz')
- marker_velocity: float32 [4096, 3, 256], P('gz')
Inputs may be any that keep to these rules, and one draw needn't show every extreme that they name: `dest_slab`: among the blocks of one device no slab is named more than 8 times.
All inputs are finite; a program needn't handle non-finite values.
Results may differ from a plain program's by a relative error of at most 0.00096.
Values may be sent and summed in bfloat16 or wider, within the bound.
A program may use at most 256 MiB of HBM per device.

v0:
```python
import functools

import jax
import jax.numpy as jnp
from jax import lax
from jax.experimental import pallas as pl
from jax.experimental.pallas import tpu as pltpu
from jax.sharding import PartitionSpec as P

CZ = 4
BOX = 16
SWEEPS = 2
CSWEEPS = 6


screening = 1.0 / 64.0
relaxation = 2.0 / 3.0


def padded_2(array, sides, width):
    for axis, dim in sides:
        size, length = (lax.axis_size(axis), array.shape[dim])
        up = [(i, (i + 1) % size) for i in range(size)]
        down = [(j, i) for i, j in up]
        last = lax.slice_in_dim(array, length - width, length, axis=dim)
        initial = lax.slice_in_dim(array, 0, width, axis=dim)
        before = lax.ppermute(last, axis, up)
        after = lax.ppermute(initial, axis, down)
        array = jnp.concatenate([before, array, after], axis=dim)
    return array


ROWS = 2 * CZ * 3
HALF = CZ * 3
PACK = 8


def marker_tables(positions):
    scale = jnp.array([BOX - 5.0, BOX - 5.0, CZ - 1.0], jnp.float32)[None, :, None]
    shift = jnp.array([2.0, 2.0, 0.0], jnp.float32)[None, :, None]
    place = shift + scale * positions
    turn = 0.5 * jnp.pi * (place - 4.0 * jnp.floor(0.25 * place))
    return jnp.concatenate([place, jnp.cos(turn), jnp.sin(turn)], axis=1)


def phi_rows(table, axis, cell):
    quarter = cell & 3
    along_cos = jnp.where(quarter == 0, 1.0, jnp.where(quarter == 2, -1.0, 0.0))
    along_sin = jnp.where(quarter == 1, 1.0, jnp.where(quarter == 3, -1.0, 0.0))
    offset = table[axis : axis + 1] - cell.astype(jnp.float32)
    wave = along_cos * table[3 + axis : 4 + axis] + along_sin * table[6 + axis : 7 + axis]
    return jnp.where(jnp.abs(offset) < 2.0, 0.25 + 0.25 * wave, 0.0)


def split_two(value):
    high = value.astype(jnp.bfloat16)
    return high, (value - high.astype(jnp.float32)).astype(jnp.bfloat16)


def block_weights(table):
    marks = table.shape[1]
    cell = lax.broadcasted_iota(jnp.int32, (BOX, marks), 0)
    weight_x = phi_rows(table, 0, cell)
    weight_y = phi_rows(table, 1, cell)
    weight_z = phi_rows(table, 2, cell & (CZ - 1))
    plane = (weight_x[:, None, :] * weight_y[None, :, :]).reshape(BOX * BOX, marks)
    return weight_z, split_two(plane)


def build_kernel(slot_ref, table_ref, force_ref, out_ref, box_ref):
    blocks, marks = table_ref.shape[0], table_ref.shape[2]
    box_ref[...] = jnp.zeros_like(box_ref)

    def one(block):
        weight_z, (plane_high, plane_low) = block_weights(table_ref[block])
        force = force_ref[block]
        row = lax.broadcasted_iota(jnp.int32, (BOX, marks), 0)
        force = jnp.where(
            row < CZ,
            force[0:1],
            jnp.where(row < 2 * CZ, force[1:2], jnp.where(row < 3 * CZ, force[2:3], 0.0)),
        )
        loaded = jnp.concatenate(split_two(weight_z * force), axis=0)
        dims = (((1,), (1,)), ((), ()))
        both = lax.dot_general(loaded, plane_high, dims, preferred_element_type=jnp.float32)
        both = both + lax.dot_general(loaded, plane_low, dims, preferred_element_type=jnp.float32)
        box = both[:BOX] + both[BOX:]
        slot = slot_ref[block]
        box_ref[slot, 0:HALF, :] = box[:HALF, :128]
        box_ref[slot, HALF:ROWS, :] = box[:HALF, 128:]

    def some(turn, carry):
        for part in range(4):
            one(turn * 4 + part)
        return carry

    lax.fori_loop(0, blocks // 4, some, 0)
    pack_boxes(box_ref, out_ref)


def pack_boxes(box_ref, out_ref):
    def pack(turn, carry):
        boxes = box_ref[pl.ds(turn * PACK, PACK)]
        out_ref[pl.ds(pl.multiple_of(turn * PACK * ROWS, PACK * ROWS), PACK * ROWS), :] = (
            boxes.reshape(PACK * ROWS, 128).astype(jnp.bfloat16)
        )
        return carry

    lax.fori_loop(0, box_ref.shape[0] // PACK, pack, 0)


def unpack_boxes(in_ref, box_ref):
    def unpack(turn, carry):
        rows = in_ref[pl.ds(pl.multiple_of(turn * PACK * ROWS, PACK * ROWS), PACK * ROWS), :]
        box_ref[pl.ds(turn * PACK, PACK)] = rows.astype(jnp.float32).reshape(PACK, ROWS, 128)
        return carry

    lax.fori_loop(0, box_ref.shape[0] // PACK, unpack, 0)


def read_kernel(slot_ref, table_ref, in_ref, out_ref, box_ref):
    blocks = table_ref.shape[0]
    unpack_boxes(in_ref, box_ref)

    def one(block):
        weight_z, (plane_high, plane_low) = block_weights(table_ref[block])
        slot = slot_ref[block]
        first = box_ref[slot, 0:BOX, :]
        second = box_ref[slot, HALF - 4 : ROWS, :]
        second = pltpu.roll(second, BOX - 4, 0)
        box = jnp.concatenate([first, second], axis=1).astype(jnp.bfloat16)
        spread = jnp.dot(box, plane_high, preferred_element_type=jnp.float32)
        spread = spread + jnp.dot(box, plane_low, preferred_element_type=jnp.float32)
        spread = spread * weight_z
        for component in range(3):
            out_ref[block, component : component + 1, :] = jnp.sum(
                spread[component * CZ : (component + 1) * CZ], axis=0, keepdims=True
            )

    def some(turn, carry):
        for part in range(4):
            one(turn * 4 + part)
        return carry

    lax.fori_loop(0, blocks // 4, some, 0)


def place_kernel(base_ref, in_ref, fluid_ref, out_ref, box_ref, grid_ref):
    slots, width = box_ref.shape[0], fluid_ref.shape[2]
    unpack_boxes(in_ref, box_ref)
    grid_ref[...] = jnp.zeros_like(grid_ref)
    lane = lax.broadcasted_iota(jnp.int32, (ROWS, 128), 1)

    def one(slot):
        first_x, first_y = base_ref[2 * slot], base_ref[2 * slot + 1]

        @pl.when(first_x >= 0)
        def _():
            box = box_ref[slot]
            inside = ((lane - first_y) & (width - 1)) < BOX
            for step in range(8):
                moved = pltpu.roll(box, (first_y - BOX * step) & (width - 1), 1)
                x = (first_x + step) & (width - 1)
                grid_ref[x] += jnp.where(inside, moved, 0.0)

    def some(turn, carry):
        for part in range(4):
            one(turn * 4 + part)
        return carry

    lax.fori_loop(0, slots // 4, some, 0)
    for layer in range(CZ):
        for component in range(3):
            row = component * CZ + layer
            near = grid_ref[:, row, :]
            far = pltpu.roll(grid_ref[:, HALF + row, :], 8, 0)
            out_ref[layer, component] = fluid_ref[layer, component] + (near + far)


def pick_kernel(base_ref, velocity_ref, out_ref, box_ref, grid_ref):
    slots, width = box_ref.shape[0], velocity_ref.shape[2]
    for layer in range(CZ):
        for component in range(3):
            row = component * CZ + layer
            low = velocity_ref[layer, component].astype(jnp.bfloat16).astype(jnp.float32)
            grid_ref[:, row, :] = low
            grid_ref[:, HALF + row, :] = pltpu.roll(low, width - 8, 0)
    lane = lax.broadcasted_iota(jnp.int32, (ROWS, 128), 1)

    def one(slot):
        first_x, first_y = base_ref[2 * slot], base_ref[2 * slot + 1]

        @pl.when(first_x < 0)
        def _():
            box_ref[slot] = jnp.zeros((ROWS, 128), jnp.float32)

        @pl.when(first_x >= 0)
        def _():
            box = jnp.zeros((ROWS, 128), jnp.float32)
            for step in range(8):
                x = (first_x + step) & (width - 1)
                moved = pltpu.roll(grid_ref[x], (BOX * step - first_y) & (width - 1), 1)
                box = jnp.where(lane // BOX == step, moved, box)
            box_ref[slot] = box

    def some(turn, carry):
        for part in range(4):
            one(turn * 4 + part)
        return carry

    lax.fori_loop(0, slots // 4, some, 0)
    pack_boxes(box_ref, out_ref)


VM = pl.BlockSpec(memory_space=pltpu.VMEM)
SM = pl.BlockSpec(memory_space=pltpu.SMEM)


def local_call(body, out, specs, scratch, name):
    return pl.pallas_call(
        body,
        out_shape=out,
        in_specs=specs,
        out_specs=VM,
        scratch_shapes=scratch,
        name=name,
        compiler_params=pltpu.CompilerParams(vmem_limit_bytes=56 * 2**20),
    )


def factor_of(level):
    return relaxation / (screening + 6.0 * 0.25**level)


def wide_dot(left, right):
    return jnp.dot(
        left, right, precision=lax.Precision.HIGHEST, preferred_element_type=jnp.float32
    )


def table(rows, columns, rule):
    row = lax.broadcasted_iota(jnp.int32, (rows, columns), 0)
    column = lax.broadcasted_iota(jnp.int32, (rows, columns), 1)
    return jnp.where(rule(row, column), 1.0, 0.0).astype(jnp.float32)


def beside(value, group_rows, group):
    axis = value.ndim - 2
    rows, lanes = value.shape[axis], value.shape[axis + 1]
    right = pltpu.roll(value, lanes - 1, axis + 1)
    left = pltpu.roll(value, 1, axis + 1)
    after = pltpu.roll(value, rows - 1, axis)
    before = pltpu.roll(value, 1, axis)
    if group < lanes:
        lane = lax.broadcasted_iota(jnp.int32, value.shape, axis + 1) & (group - 1)
        row = lax.broadcasted_iota(jnp.int32, value.shape, axis) & (group_rows - 1)
        right = jnp.where(lane == group - 1, pltpu.roll(value, group - 1, axis + 1), right)
        left = jnp.where(lane == 0, pltpu.roll(value, lanes - group + 1, axis + 1), left)
        wrap_after, wrap_before = after, before
        if group_rows < rows:
            wrap_after = pltpu.roll(value, group_rows - 1, axis)
            wrap_before = pltpu.roll(value, rows - group_rows + 1, axis)
        after = jnp.where(
            row == group_rows - 1, pltpu.roll(wrap_after, lanes - group, axis + 1), after
        )
        before = jnp.where(row == 0, pltpu.roll(wrap_before, group, axis + 1), before)
    return (right + left) + (after + before)


def first_sweep(source, around, level):
    factor = factor_of(level)
    return (4.0 / 3.0 * factor) * source + (factor * factor * 0.25**level) * around


def next_sweep(solution, source, around, level):
    factor = factor_of(level)
    return (1.0 - relaxation) * solution + factor * source + (factor * 0.25**level) * around


def left_over(solution, source, around, level):
    return source - (screening + 6.0 * 0.25**level) * solution + 0.25**level * around


def grid_kernel(
    devices,
    source_ref,
    out_ref,
    b0,
    u0,
    t0,
    b1,
    u1,
    t1,
    f1,
    b2,
    u2,
    send0,
    recv0,
    send1,
    recv1,
    send2,
    recv2,
):
    me = lax.axis_index("gz")

    def other(step):
        return lax.rem(me + step + devices, devices)

    barrier = pltpu.get_barrier_semaphore()

    def greet(step, carry):
        pl.semaphore_signal(
            barrier, inc=1, device_id=(other(step),), device_id_type=pl.DeviceIdType.MESH
        )
        return carry

    lax.fori_loop(1, devices, greet, 0)
    pl.semaphore_wait(barrier, devices - 1)

    def send(src, dst, send_sem, recv_sem, step):
        copy = pltpu.make_async_remote_copy(
            src_ref=src,
            dst_ref=dst,
            send_sem=send_sem,
            recv_sem=recv_sem,
            device_id=(other(step),),
            device_id_type=pl.DeviceIdType.MESH,
        )
        copy.start()
        return copy

    width, lanes = source_ref.shape[2], source_ref.shape[3]
    near = [
        send(source_ref.at[2:4], b0.at[1:3], send0.at[0], recv0.at[0], 1),
        send(source_ref.at[0:2], b0.at[7:9], send0.at[1], recv0.at[1], -1),
    ]
    far = [
        send(source_ref.at[1:2], b0.at[0:1], send0.at[2], recv0.at[2], 1),
        send(source_ref.at[2:3], b0.at[9:10], send0.at[3], recv0.at[3], -1),
    ]

    def loop(low, high, body):
        def step(turn, carry):
            for component in range(3):
                body(turn, component)
            return carry

        lax.fori_loop(low, high, step, 0)

    def keep(z, c):
        b0[z + 3, c] = source_ref[z, c]

    loop(0, 4, keep)

    def begin0(z, c):
        here = b0[z, c]
        around = beside(here, width, lanes) + (b0[z - 1, c] + b0[z + 1, c])
        u0[z - 1, c] = first_sweep(here, around, 0)

    loop(4, 6, begin0)
    for copy in near:
        copy.wait()
    loop(2, 4, begin0)
    loop(6, 8, begin0)

    half = width // 2
    fold0 = table(half, width, lambda r, c: c // 2 == r)
    pack0 = [
        table(lanes, lanes, lambda r, c, a=a: (c // half == a) & (r // 2 == c % half))
        for a in range(2)
    ]
    quarter = half // 2
    fold1 = table(quarter // 2, quarter, lambda r, c: c // 2 == r)
    rows1, rows2 = quarter, quarter // 4
    group1, group2 = half, quarter

    def rest0(z, c):
        here = u0[z + 2, c]
        around = beside(here, width, lanes) + (u0[z + 1, c] + u0[z + 3, c])
        return left_over(here, b0[z + 3, c], around, 0)

    def down0(z1, c):
        pair = 0.125 * (rest0(2 * z1, c) + rest0(2 * z1 + 1, c))
        folded = wide_dot(fold0, pair)
        b1[z1 + 4, c] = wide_dot(folded[:rows1], pack0[0]) + wide_dot(folded[rows1:], pack0[1])

    loop(0, 2, down0)
    near1 = [
        send(b1.at[4:6], b1.at[2:4], send1.at[0], recv1.at[0], 1),
        send(b1.at[4:6], b1.at[6:8], send1.at[1], recv1.at[1], -1),
    ]
    far1 = [
        send(b1.at[4:6], b1.at[0:2], send1.at[2], recv1.at[2], 2),
        send(b1.at[4:6], b1.at[8:10], send1.at[3], recv1.at[3], -2),
    ]

    def begin1(z, c):
        here = b1[z, c]
        around = beside(here, rows1, group1) + (b1[z - 1, c] + b1[z + 1, c])
        u1[z - 1, c] = first_sweep(here, around, 1)

    for copy in near1:
        copy.wait()
    loop(3, 7, begin1)

    def rest1(z, c):
        here = u1[z + 3, c]
        around = beside(here, rows1, group1) + (u1[z + 2, c] + u1[z + 4, c])
        return left_over(here, b1[z + 4, c], around, 1)

    pack1 = [
        table(
            lanes,
            lanes,
            lambda r, c, a=a: (c // group2 == 2 * (r // group1) + a)
            & (c % group2 == (r % group1) // 2),
        )
        for a in range(2)
    ]
    for c in range(3):
        folded = wide_dot(fold1, 0.125 * (rest1(0, c) + rest1(1, c)))
        b2[me, c] = wide_dot(folded[:rows2], pack1[0]) + wide_dot(folded[rows2:], pack1[1])

    def spread(step, carry):
        send(b2.at[me], b2.at[me], send2, recv2, step)
        return carry

    lax.fori_loop(1, devices, spread, 0)
    for copy in far:
        copy.wait()
    loop(1, 2, begin0)
    loop(8, 9, begin0)
    for copy in far1:
        copy.wait()
    loop(1, 3, begin1)
    loop(7, 9, begin1)
    rest = b2.at[0 : devices - 1]
    pltpu.make_async_copy(rest, rest, send2).wait()
    pltpu.make_async_copy(rest, rest, recv2).wait()

    count = 3 * devices
    half2 = devices // 2
    group3 = group2 // 2
    rhs2 = b2[...].reshape(count, rows2, lanes)

    def around2(value):
        ends = jnp.concatenate([value[3:], value[:3]], 0) + jnp.concatenate(
            [value[-3:], value[:-3]], 0
        )
        return beside(value, rows2, group2) + ends

    sol2 = first_sweep(rhs2, around2(rhs2), 2)
    left2 = left_over(sol2, rhs2, around2(sol2), 2).reshape(half2, 2, 3 * rows2, lanes)
    left2 = (0.125 * (left2[:, 0] + left2[:, 1])).reshape(half2 * 3 * rows2, lanes)
    span3 = 4 * group3
    pack2 = table(
        lanes,
        lanes,
        lambda r, c: ((c % span3) // group3 == r // group2) & (c % group3 == (r % group2) // 2),
    )
    rows3 = rows2 // 2
    fold2 = table(
        4 * rows3,
        3 * rows2,
        lambda r, c: (c // rows2 == r // rows3) & ((c % rows2) // 2 == r % rows3),
    )
    left2 = wide_dot(left2, pack2).reshape(half2, 3 * rows2, lanes)
    rhs3 = jnp.stack([wide_dot(fold2, left2[z]) for z in range(half2)], 0)

    def around3(value):
        ends = jnp.concatenate([value[1:], value[:1]], 0) + jnp.concatenate(
            [value[-1:], value[:-1]], 0
        )
        return beside(value, rows3, group3) + ends

    sol3 = first_sweep(rhs3, around3(rhs3), 3)
    for turn in range(CSWEEPS - 2):
        sol3 = next_sweep(sol3, rhs3, around3(sol3), 3)
    total = jnp.sum(left_over(sol3, rhs3, around3(sol3), 3), axis=0)
    total = jnp.broadcast_to(jnp.sum(total, axis=1, keepdims=True), total.shape)
    same = table(4 * rows3, 4 * rows3, lambda r, c: r // rows3 == c // rows3)
    cells = half2 * rows3 * lanes
    sol3 = sol3 + (wide_dot(same, total) * (1.0 / (screening * cells)))[None]

    open2 = table(
        lanes,
        lanes,
        lambda r, c: (r < span3)
        & (r // group3 == c // group2)
        & (r % group3 == (c % group2) // 2),
    )
    rise2 = table(
        3 * rows2,
        4 * rows3,
        lambda r, c: (r // rows2 == c // rows3) & ((r % rows2) // 2 == c % rows3),
    )
    lift = jnp.concatenate([wide_dot(rise2, sol3[z]) for z in range(half2)], 0)
    lift = wide_dot(lift, open2).reshape(half2, 1, 3 * rows2, lanes)
    lift = jnp.concatenate([lift, lift], axis=1).reshape(count, rows2, lanes)
    sol2 = sol2 + lift
    for turn in range(SWEEPS):
        sol2 = next_sweep(sol2, rhs2, around2(sol2), 2)
    u2[...] = sol2.reshape(devices, 3, rows2, lanes)

    rise1 = table(quarter, quarter // 2, lambda r, c: r // 2 == c)
    open1 = [
        table(
            lanes,
            lanes,
            lambda r, c, a=a: (r // group2 == 2 * (c // group1) + a)
            & (r % group2 == (c % group1) // 2),
        )
        for a in range(2)
    ]

    def lift1(z2, c):
        coarse = u2[other(z2 - 2), c]
        tall = jnp.concatenate([wide_dot(coarse, open1[0]), wide_dot(coarse, open1[1])], 0)
        return wide_dot(rise1, tall)

    for c in range(3):
        u1[0, c] += lift1(0, c)
        u1[7, c] += lift1(4, c)

    def raise1(z2, c):
        up = lift1(z2, c)
        u1[2 * z2 - 1, c] += up
        u1[2 * z2, c] += up

    loop(1, 4, raise1)

    def later1(z, c):
        here = u1[z, c]
        around = beside(here, rows1, group1) + (u1[z - 1, c] + u1[z + 1, c])
        t1[z - 1, c] = next_sweep(here, b1[z + 1, c], around, 1)

    loop(1, 7, later1)

    def last1(z, c):
        here = t1[z, c]
        around = beside(here, rows1, group1) + (t1[z - 1, c] + t1[z + 1, c])
        f1[z - 1, c] = next_sweep(here, b1[z + 2, c], around, 1)

    loop(1, 5, last1)

    rise0 = table(width, half, lambda r, c: r // 2 == c)
    open0 = [
        table(lanes, lanes, lambda r, c, a=a: (r // half == a) & (c // 2 == r % half))
        for a in range(2)
    ]

    def raise0(z1, c):
        coarse = f1[z1, c]
        tall = jnp.concatenate([wide_dot(coarse, open0[0]), wide_dot(coarse, open0[1])], 0)
        up = wide_dot(rise0, tall)
        u0[2 * z1, c] += up
        u0[2 * z1 + 1, c] += up

    loop(0, 4, raise0)

    def later0(z, c):
        here = u0[z, c]
        around = beside(here, width, lanes) + (u0[z - 1, c] + u0[z + 1, c])
        t0[z - 1, c] = next_sweep(here, b0[z + 1, c], around, 0)

    loop(1, 7, later0)

    def last0(z, c):
        here = t0[z, c]
        around = beside(here, width, lanes) + (t0[z - 1, c] + t0[z + 1, c])
        out_ref[z - 1, c] = next_sweep(here, b0[z + 2, c], around, 0)

    loop(1, 5, last0)


def multigrid(source):
    devices = lax.axis_size("gz")
    width = source.shape[3]
    fine, middle, third = (3, width, width), (3, width // 4, width), (3, width // 16, width)
    dma = pltpu.SemaphoreType.DMA
    scratch = [
        pltpu.VMEM((10,) + fine, jnp.float32),
        pltpu.VMEM((8,) + fine, jnp.float32),
        pltpu.VMEM((6,) + fine, jnp.float32),
        pltpu.VMEM((10,) + middle, jnp.float32),
        pltpu.VMEM((8,) + middle, jnp.float32),
        pltpu.VMEM((6,) + middle, jnp.float32),
        pltpu.VMEM((4,) + middle, jnp.float32),
        pltpu.VMEM((devices,) + third, jnp.float32),
        pltpu.VMEM((devices,) + third, jnp.float32),
        dma((4,)),
        dma((4,)),
        dma((4,)),
        dma((4,)),
        dma,
        dma,
    ]
    return pl.pallas_call(
        functools.partial(grid_kernel, devices),
        out_shape=jax.ShapeDtypeStruct(source.shape, jnp.float32),
        in_specs=[VM],
        out_specs=VM,
        scratch_shapes=scratch,
        name="multigrid",
        compiler_params=pltpu.CompilerParams(
            collective_id=0, has_side_effects=True, vmem_limit_bytes=56 * 2**20
        ),
    )(source)


def shards(marker_positions, marker_forces, dest_slab, base_cells, fluid_source):
    devices = lax.axis_size("gz")
    held_blocks = marker_positions.shape[0]
    width = fluid_source.shape[2]
    capacity = max(2, 2 * held_blocks // devices)
    slots = devices * capacity
    target = dest_slab[:, 0]
    dest_hits = (target[:, None] == jnp.arange(devices, dtype=jnp.int32)[None, :]).astype(jnp.int32)
    earlier = jnp.arange(held_blocks)[:, None] > jnp.arange(held_blocks)[None, :]
    slot_order = jnp.sum((earlier & (target[:, None] == target[None, :])).astype(jnp.int32), axis=1)
    slot_index = target * capacity + slot_order
    slot_hits = slot_index[None, :] == jnp.arange(slots, dtype=jnp.int32)[:, None]
    base_sent = jnp.sum(
        jnp.where(slot_hits[:, :, None], base_cells[None, :, :] + 1, 0), axis=1
    )
    arrived_base = lax.all_to_all(
        base_sent.reshape(devices, capacity * 2), "gz", split_axis=0, concat_axis=0, tiled=True
    )
    arrived_base = arrived_base.reshape(-1) - 1
    tables = marker_tables(marker_positions)
    boxes = pltpu.VMEM((slots, ROWS, 128), jnp.float32)
    grid = pltpu.VMEM((width, ROWS, 128), jnp.float32)
    packed = jax.ShapeDtypeStruct((slots * ROWS, 128), jnp.bfloat16)
    box_sent = local_call(build_kernel, packed, [SM, VM, VM], [boxes], "build")(
        slot_index, tables, marker_forces
    )
    arrived = lax.all_to_all(box_sent, "gz", split_axis=0, concat_axis=0, tiled=True)
    source = local_call(
        place_kernel,
        jax.ShapeDtypeStruct(fluid_source.shape, jnp.float32),
        [SM, VM, VM],
        [boxes, grid],
        "place",
    )(arrived_base, arrived, fluid_source)
    velocity = multigrid(source)
    picked = local_call(pick_kernel, packed, [SM, VM], [boxes, grid], "pick")(
        arrived_base, velocity
    )
    returned = lax.all_to_all(picked, "gz", split_axis=0, concat_axis=0, tiled=True)
    marker_velocity = local_call(
        read_kernel,
        jax.ShapeDtypeStruct(marker_positions.shape, jnp.float32),
        [SM, VM, VM],
        [boxes],
        "read",
    )(slot_index, tables, returned)
    return (velocity, marker_velocity)


def solution(mesh):
    placed = (
        P("gz", None, None),
        P("gz", None, None),
        P("gz", None),
        P("gz", None),
        P("gz", None, None, None),
    )
    return jax.shard_map(
        shards,
        mesh=mesh,
        in_specs=placed,
        out_specs=(P("gz", None, None, None), P("gz", None, None)),
        check_vma=False,
    )
```

profile of v0, /device:TPU:0, one launch (start us, length us, event | category | flops | bytes accessed | tf_op | source)
XLA Modules:
  0.0 257.0 jit_solution(16087272052223736389)
XLA Ops:
  0.6 0.9 convert_reduce_fusion
  1.5 0.7 multiply_add_fusion.slot_ref
  2.2 0.7 broadcast_add_fusion
  2.9 0.1 select_reduce_fusion
  3.1 0.1 copy.27
  3.2 0.7 all_to_all.20
  3.9 7.3 %all-to-all-start = ((s32[32,1,16]{2,1,0:T(1,128)}), s32[32,1,16]{2,1,0:T(1,128)S(1)}, u32[]{:S(2)}, u32[]{:S(2)}) async-start(s32[32,1,16]{2,1,0:T(1,128)} %bitcast.1), calls=%async_computation | async-start | bytes 32768 | tf_op jit(solution)/shard_map/all_to_all | solution.py:626
  11.3 4.9 %fusion.2 = (f32[128,3,256]{2,1,0:T(4,128)S(1)}, f32[128,3,256]{2,1,0:T(4,128)S(1)}) fusion(f32[128,3,256]{2,0,1:T(8,128)} %param.7, f32[3]{0:T(128)} %constant.19.clone, f32[3]{0:T(128)} %constant.20.clone), kind=kLoop, calls=%fused_computation.6 | loop fusion | flops 688128 | bytes 1179672 | tf_op jit(solution)/shard_map/cos | solution.py:43
  16.2 3.6 %fusion.1 = f32[128,3,256]{2,1,0:T(4,128)S(1)} fusion(f32[128,3,256]{2,1,0:T(4,128)S(1)} %get-tuple-element.13), kind=kLoop, calls=%fused_computation.5 | loop fusion | flops 491520 | bytes 786432 | tf_op jit(solution)/shard_map/sin | solution.py:43
  19.8 0.0 copy-start.2
  19.8 1.9 pad_maximum_fusion.table_ref
  21.7 1.1 copy.31.force_ref
  22.7 18.5 %build.1 = bf16[6144,128]{1,0:T(8,128)(2,1)} custom-call(s32[128]{0:T(128)} %copy-done.3, f32[128,9,256]{2,1,0:T(8,128)} %pad_maximum_fusion.table_ref, f32[128,3,256]{2,1,0:T(4,128)} %copy.31.force_ref), custom_call_target="tpu_custom_call" | custom-call | tf_op jit(solution)/shard_map/build/pallas_call | solution.py:634
  41.3 6.0 %all-to-all-start.1 = ((bf16[32,192,128]{2,1,0:T(8,128)(2,1)}), bf16[32,192,128]{2,1,0:T(8,128)(2,1)S(1)}, u32[]{:S(2)}, u32[]{:S(2)}) async-start(bf16[32,192,128]{2,1,0:T(8,128)(2,1)} %bitcast.7), calls=%async_computation.1 | async-start | bytes 3145728 | tf_op jit(solution)/shard_map/all_to_all | solution.py:637
  47.3 0.7 sub.10.base_ref
  48.0 36.8 %all-to-all-done.1 = bf16[32,192,128]{2,1,0:T(8,128)(2,1)S(1)} async-done(((bf16[32,192,128]{2,1,0:T(8,128)(2,1)}), bf16[32,192,128]{2,1,0:T(8,128)(2,1)S(1)}, u32[]{:S(2)}, u32[]{:S(2)}) %all-to-all-start.1) | async-done | bytes 1572896 | tf_op jit(solution)/shard_map/all_to_all | solution.py:637
  84.8 1.1 copy-done.1
  85.9 15.9 %place.1.source_ref = f32[4,3,128,128]{3,2,1,0:T(8,128)} custom-call(s32[512]{0:T(512)} %sub.10.base_ref, bf16[6144,128]{1,0:T(8,128)(2,1)} %bitcast.9, f32[4,3,128,128]{3,2,1,0:T(8,128)} %fluid_ref.1), custom_call_target="tpu_custom_call" | custom-call | tf_op jit(solution)/shard_map/place/pallas_call | solution.py:638
  101.9 64.3 %multigrid.1.velocity_ref = f32[4,3,128,128]{3,2,1,0:T(8,128)} custom-call(f32[4,3,128,128]{3,2,1,0:T(8,128)} %place.1.source_ref), custom_call_target="tpu_custom_call" | custom-call | tf_op jit(solution)/shard_map/multigrid/pallas_call | solution.py:598
  166.1 15.3 %pick.1 = bf16[6144,128]{1,0:T(8,128)(2,1)} custom-call(s32[512]{0:T(512)} %sub.10.base_ref, f32[4,3,128,128]{3,2,1,0:T(8,128)} %multigrid.1.velocity_ref), custom_call_target="tpu_custom_call" | custom-call | tf_op jit(solution)/shard_map/pick/pallas_call | solution.py:646
  181.5 57.1 %all_to_all.31 = bf16[32,192,128]{2,1,0:T(8,128)(2,1)} all-to-all(bf16[32,192,128]{2,1,0:T(8,128)(2,1)} %bitcast.10), channel_id=1, replica_groups=mesh['gz'=32] {'gz'}, dimensions={0} | all-to-all | bytes 3145728 | tf_op jit(solution)/shard_map/all_to_all | solution.py:649
  238.5 15.8 %read.1 = f32[128,3,256]{2,1,0:T(4,128)} custom-call(s32[128]{0:T(128)} %copy-done.3, f32[128,9,256]{2,1,0:T(8,128)} %pad_maximum_fusion.table_ref, bf16[6144,128]{1,0:T(8,128)(2,1)} %bitcast.8), custom_call_target="tpu_custom_call" | custom-call | tf_op jit(solution)/shard_map/read/pallas_call | solution.py:650
  254.3 1.9 copy.32
  256.2 0.9 copy.38
  (9 shorter events, 0.1 us)
Async XLA Ops:
  2.2 19.5 %copy-start.3 = (s32[128]{0:T(128)}, s32[128]{0:T(128)S(1)}, u32[]{:S(2)}) copy-start(s32[128]{0:T(128)S(1)} %multiply_add_fusion.slot_ref) | copy-start | bytes 1540
  3.9 37.3 %all-to-all-start = ((s32[32,1,16]{2,1,0:T(1,128)}), s32[32,1,16]{2,1,0:T(1,128)S(1)}, u32[]{:S(2)}, u32[]{:S(2)}) async-start(s32[32,1,16]{2,1,0:T(1,128)} %bitcast.1), calls=%async_computation | async-start | bytes 32768 | tf_op jit(solution)/shard_map/all_to_all | solution.py:626
  19.8 1.9 copy-start.2
  41.3 43.5 %all-to-all-start.1 = ((bf16[32,192,128]{2,1,0:T(8,128)(2,1)}), bf16[32,192,128]{2,1,0:T(8,128)(2,1)S(1)}, u32[]{:S(2)}, u32[]{:S(2)}) async-start(bf16[32,192,128]{2,1,0:T(8,128)(2,1)} %bitcast.7), calls=%async_computation.1 | async-start | bytes 3145728 | tf_op jit(solution)/shard_map/all_to_all | solution.py:637
  84.8 1.1 copy-start.1
  238.5 17.6 %copy-start = (f32[4,3,128,128]{3,2,1,0:T(8,128)S(1)}, f32[4,3,128,128]{3,2,1,0:T(8,128)}, u32[]{:S(2)}) copy-start(f32[4,3,128,128]{3,2,1,0:T(8,128)} %multigrid.1.velocity_ref) | copy-start | bytes 2359300
where the time goes:
time: 257 us
  Pallas kernels  130 us (51%)
  blocking collectives  57.1 us (22%)
  waiting for transfers between devices  36.8 us (14%)
  starting transfers between devices  13.3 us (5%)
  other arithmetic  12.9 us (5%)
  local copies, waits for them, and re-layouts  6.47 us (3%)
    pallas_call x1, Pallas kernels, multigrid(): pl.pallas_call(functools.partial(grid_kernel, devices), out_shape=jax.Sha...  64.3 us
    all_to_all x1, blocking collectives, shards(): lax.all_to_all(picked, 'gz', split_axis=0, concat_axis=0, tiled=True)  57.1 us
    all_to_all x1, waiting for transfers between devices, shards(): lax.all_to_all(box_sent, 'gz', split_axis=0, concat_axis=0, tiled=True)  36.8 us
    pallas_call x1, Pallas kernels, shards(): local_call(build_kernel, packed, [SM, VM, VM], [boxes], 'build')  18.5 us
    pallas_call x1, Pallas kernels, shards(): local_call(place_kernel, jax.ShapeDtypeStruct(fluid_source.shape, jnp.flo...  15.9 us
    pallas_call x1, Pallas kernels, shards(): local_call(read_kernel, jax.ShapeDtypeStruct(marker_positions.shape, jnp....  15.8 us
    pallas_call x1, Pallas kernels, shards(): local_call(pick_kernel, packed, [SM, VM], [boxes, grid], 'pick')  15.3 us
    all_to_all x1, starting transfers between devices, shards(): lax.all_to_all(base_sent.reshape(devices, capacity * 2), 'gz', split_axis...  7.33 us
  transfers between devices with their start and end apart: 2, of which 1 were waited for; matrix products, arithmetic and copies ran while one was open for 5% of the time, Pallas kernels for 7%

commit v1 on v0

--- a/solution.py
+++ b/solution.py
@@ -1,4 +1,5 @@
 import functools
+import math
 
 import jax
 import jax.numpy as jnp
@@ -35,12 +36,29 @@
 PACK = 8
 
 
+def series(value, terms):
+    total = jnp.full_like(value, terms[-1])
+    for term in terms[-2::-1]:
+        total = term + value * total
+    return total
+
+
 def marker_tables(positions):
     scale = jnp.array([BOX - 5.0, BOX - 5.0, CZ - 1.0], jnp.float32)[None, :, None]
     shift = jnp.array([2.0, 2.0, 0.0], jnp.float32)[None, :, None]
     place = shift + scale * positions
-    turn = 0.5 * jnp.pi * (place - 4.0 * jnp.floor(0.25 * place))
-    return jnp.concatenate([place, jnp.cos(turn), jnp.sin(turn)], axis=1)
+    nearest = jnp.floor(place + 0.5)
+    turn = 0.5 * jnp.pi * (place - nearest)
+    square = turn * turn
+    cosine = series(square, [(-1.0) ** n / math.factorial(2 * n) for n in range(6)])
+    sine = turn * series(square, [(-1.0) ** n / math.factorial(2 * n + 1) for n in range(6)])
+    quarter = nearest.astype(jnp.int32) & 3
+    odd = (quarter & 1) == 1
+    along_cos = jnp.where(odd, sine, cosine)
+    along_sin = jnp.where(odd, cosine, sine)
+    along_cos = jnp.where((quarter == 1) | (quarter == 2), -along_cos, along_cos)
+    along_sin = jnp.where(quarter >= 2, -along_sin, along_sin)
+    return jnp.concatenate([place, along_cos, along_sin], axis=1)
 
 
 def phi_rows(table, axis, cell):
@@ -67,7 +85,7 @@
     return weight_z, split_two(plane)
 
 
-def build_kernel(slot_ref, table_ref, force_ref, out_ref, box_ref):
+def build_kernel(slot_ref, base_ref, table_ref, force_ref, out_ref, box_ref):
     blocks, marks = table_ref.shape[0], table_ref.shape[2]
     box_ref[...] = jnp.zeros_like(box_ref)
 
@@ -86,7 +104,14 @@
         both = both + lax.dot_general(loaded, plane_low, dims, preferred_element_type=jnp.float32)
         box = both[:BOX] + both[BOX:]
         slot = slot_ref[block]
-        box_ref[slot, 0:HALF, :] = box[:HALF, :128]
+        near = box[:HALF, :128]
+        tile_row = lax.broadcasted_iota(jnp.int32, near.shape, 0)
+        lane = lax.broadcasted_iota(jnp.int32, near.shape, 1)
+        first_x = base_ref[2 * block].astype(jnp.float32)
+        first_y = base_ref[2 * block + 1].astype(jnp.float32)
+        near = jnp.where((tile_row == 0) & (lane == 0), first_x, near)
+        near = jnp.where((tile_row == 0) & (lane == 1), first_y, near)
+        box_ref[slot, 0:HALF, :] = near
         box_ref[slot, HALF:ROWS, :] = box[:HALF, 128:]
 
     def some(turn, carry):
@@ -145,35 +170,41 @@
     lax.fori_loop(0, blocks // 4, some, 0)
 
 
-def place_kernel(base_ref, in_ref, fluid_ref, out_ref, box_ref, grid_ref):
+def place_kernel(base_ref, in_ref, fluid_ref, out_ref, box_ref, grid_ref, twin_ref):
     slots, width = box_ref.shape[0], fluid_ref.shape[2]
     unpack_boxes(in_ref, box_ref)
     grid_ref[...] = jnp.zeros_like(grid_ref)
+    twin_ref[...] = jnp.zeros_like(twin_ref)
     lane = lax.broadcasted_iota(jnp.int32, (ROWS, 128), 1)
-
-    def one(slot):
+    row = lax.broadcasted_iota(jnp.int32, (ROWS, 128), 0)
+    label = (row == 0) & (lane < 2)
+
+    def moved_box(slot):
         first_x, first_y = base_ref[2 * slot], base_ref[2 * slot + 1]
-
-        @pl.when(first_x >= 0)
-        def _():
-            box = box_ref[slot]
-            inside = ((lane - first_y) & (width - 1)) < BOX
-            for step in range(8):
-                moved = pltpu.roll(box, (first_y - BOX * step) & (width - 1), 1)
-                x = (first_x + step) & (width - 1)
-                grid_ref[x] += jnp.where(inside, moved, 0.0)
+        box = jnp.where(label, 0.0, box_ref[slot])
+        inside = ((lane - first_y) & (width - 1)) < BOX
+        pieces = []
+        for step in range(8):
+            moved = pltpu.roll(box, (first_y - BOX * step) & (width - 1), 1)
+            pieces.append(((first_x + step) & (width - 1), jnp.where(inside, moved, 0.0)))
+        return pieces
 
     def some(turn, carry):
-        for part in range(4):
-            one(turn * 4 + part)
+        for part in range(2):
+            even = moved_box(4 * turn + 2 * part)
+            odd = moved_box(4 * turn + 2 * part + 1)
+            for (x, piece), (other_x, other_piece) in zip(even, odd):
+                grid_ref[x] += piece
+                twin_ref[other_x] += other_piece
         return carry
 
     lax.fori_loop(0, slots // 4, some, 0)
     for layer in range(CZ):
         for component in range(3):
             row = component * CZ + layer
-            near = grid_ref[:, row, :]
-            far = pltpu.roll(grid_ref[:, HALF + row, :], 8, 0)
+            near = grid_ref[:, row, :] + twin_ref[:, row, :]
+            far = grid_ref[:, HALF + row, :] + twin_ref[:, HALF + row, :]
+            far = pltpu.roll(far, 8, 0)
             out_ref[layer, component] = fluid_ref[layer, component] + (near + far)
 
 
@@ -190,18 +221,12 @@
     def one(slot):
         first_x, first_y = base_ref[2 * slot], base_ref[2 * slot + 1]
 
-        @pl.when(first_x < 0)
-        def _():
-            box_ref[slot] = jnp.zeros((ROWS, 128), jnp.float32)
-
-        @pl.when(first_x >= 0)
-        def _():
-            box = jnp.zeros((ROWS, 128), jnp.float32)
-            for step in range(8):
-                x = (first_x + step) & (width - 1)
-                moved = pltpu.roll(grid_ref[x], (BOX * step - first_y) & (width - 1), 1)
-                box = jnp.where(lane // BOX == step, moved, box)
-            box_ref[slot] = box
+        box = jnp.zeros((ROWS, 128), jnp.float32)
+        for step in range(8):
+            x = (first_x + step) & (width - 1)
+            moved = pltpu.roll(grid_ref[x], (BOX * step - first_y) & (width - 1), 1)
+            box = jnp.where(lane // BOX == step, moved, box)
+        box_ref[slot] = box
 
     def some(turn, carry):
         for part in range(4):
@@ -232,16 +257,26 @@
     return relaxation / (screening + 6.0 * 0.25**level)
 
 
+def split_three(value):
+    high = value.astype(jnp.bfloat16)
+    rest = value - high.astype(jnp.float32)
+    middle = rest.astype(jnp.bfloat16)
+    low = (rest - middle.astype(jnp.float32)).astype(jnp.bfloat16)
+    return [high, middle, low]
+
+
 def wide_dot(left, right):
-    return jnp.dot(
-        left, right, precision=lax.Precision.HIGHEST, preferred_element_type=jnp.float32
-    )
+    if right.dtype == jnp.bfloat16:
+        parts = [jnp.dot(p, right, preferred_element_type=jnp.float32) for p in split_three(left)]
+    else:
+        parts = [jnp.dot(left, p, preferred_element_type=jnp.float32) for p in split_three(right)]
+    return (parts[2] + parts[1]) + parts[0]
 
 
 def table(rows, columns, rule):
     row = lax.broadcasted_iota(jnp.int32, (rows, columns), 0)
     column = lax.broadcasted_iota(jnp.int32, (rows, columns), 1)
-    return jnp.where(rule(row, column), 1.0, 0.0).astype(jnp.float32)
+    return jnp.where(rule(row, column), 1.0, 0.0).astype(jnp.bfloat16)
 
 
 def beside(value, group_rows, group):
@@ -615,31 +650,24 @@
     capacity = max(2, 2 * held_blocks // devices)
     slots = devices * capacity
     target = dest_slab[:, 0]
-    dest_hits = (target[:, None] == jnp.arange(devices, dtype=jnp.int32)[None, :]).astype(jnp.int32)
     earlier = jnp.arange(held_blocks)[:, None] > jnp.arange(held_blocks)[None, :]
     slot_order = jnp.sum((earlier & (target[:, None] == target[None, :])).astype(jnp.int32), axis=1)
     slot_index = target * capacity + slot_order
-    slot_hits = slot_index[None, :] == jnp.arange(slots, dtype=jnp.int32)[:, None]
-    base_sent = jnp.sum(
-        jnp.where(slot_hits[:, :, None], base_cells[None, :, :] + 1, 0), axis=1
-    )
-    arrived_base = lax.all_to_all(
-        base_sent.reshape(devices, capacity * 2), "gz", split_axis=0, concat_axis=0, tiled=True
-    )
-    arrived_base = arrived_base.reshape(-1) - 1
     tables = marker_tables(marker_positions)
     boxes = pltpu.VMEM((slots, ROWS, 128), jnp.float32)
     grid = pltpu.VMEM((width, ROWS, 128), jnp.float32)
     packed = jax.ShapeDtypeStruct((slots * ROWS, 128), jnp.bfloat16)
-    box_sent = local_call(build_kernel, packed, [SM, VM, VM], [boxes], "build")(
-        slot_index, tables, marker_forces
+    box_sent = local_call(build_kernel, packed, [SM, SM, VM, VM], [boxes], "build")(
+        slot_index, base_cells.reshape(-1), tables, marker_forces
     )
     arrived = lax.all_to_all(box_sent, "gz", split_axis=0, concat_axis=0, tiled=True)
+    labels = lax.slice(arrived.reshape(slots, ROWS, 128), (0, 0, 0), (slots, 1, 2))
+    arrived_base = labels.reshape(-1).astype(jnp.int32)
     source = local_call(
         place_kernel,
         jax.ShapeDtypeStruct(fluid_source.shape, jnp.float32),
         [SM, VM, VM],
-        [boxes, grid],
+        [boxes, grid, grid],
         "place",
     )(arrived_base, arrived, fluid_source)
     velocity = multigrid(source)

time: 257 us -> 218 us (0.85)
  waiting for transfers between devices: 36.8 us -> 0 us
  blocking collectives: 57.1 us -> 91.1 us
  Pallas kernels: 130 us -> 110 us
  starting transfers between devices: 13.3 us -> 0 us
  other arithmetic: 12.9 us -> 8.01 us
    all_to_all x0 -> x1, blocking collectives: none -> 45.4 us  [shards(): lax.all_to_all(box_sent, 'gz', split_axis=0, concat_axis=0, tiled=True)]
    all_to_all x2 -> x0, waiting for transfers between devices: 36.8 us -> none  [the longest x1 36.8 us: shards(): lax.all_to_all(box_sent, 'gz', split_axis=0, concat_axis=0, tiled=True)]
    pallas_call x1, Pallas kernels: 64.3 us -> 46.4 us  [multigrid(): pl.pallas_call(functools.partial(grid_kernel, devices), out_shape=jax.Sha...]
    all_to_all x2 -> x0, starting transfers between devices: 13.3 us -> none  [the longest x1 7.33 us: shards(): lax.all_to_all(base_sent.reshape(devices, capacity * 2), 'gz', split_axis...]
    all_to_all x1, blocking collectives: 57.1 us -> 45.6 us  [shards(): lax.all_to_all(picked, 'gz', split_axis=0, concat_axis=0, tiled=True)]
    cos x1 -> x0, other arithmetic: 4.91 us -> none  [marker_tables(): return jnp.concatenate([place, jnp.cos(turn), jnp.sin(turn)], axis=1)]
    select_n x0 -> x2, other arithmetic: none -> 3.62 us  [the longest x1 2.43 us: marker_tables(): jnp.where((quarter == 1) | (quarter == 2), -along_cos, along_cos)]
    sin x1 -> x0, other arithmetic: 3.6 us -> none  [marker_tables(): return jnp.concatenate([place, jnp.cos(turn), jnp.sin(turn)], axis=1)]
  transfers between devices with their start and end apart: 2 -> 0, of which waited for: 1 -> 0; matrix products, arithmetic and copies ran while one was open for 5% -> 0% of each run, Pallas kernels for 7% -> 0%
where the time goes in v1:
time: 218 us; the launch traced here: 217 us
  Pallas kernels  110 us (50%)
  blocking collectives  91.1 us (42%)
  other arithmetic  8.01 us (4%)
  local copies, waits for them, and re-layouts  7.02 us (3%)
    pallas_call x1, Pallas kernels, multigrid(): pl.pallas_call(functools.partial(grid_kernel, devices), out_shape=jax.Sha...  46.4 us
    all_to_all x1, blocking collectives, shards(): lax.all_to_all(picked, 'gz', split_axis=0, concat_axis=0, tiled=True)  45.6 us
    all_to_all x1, blocking collectives, shards(): lax.all_to_all(box_sent, 'gz', split_axis=0, concat_axis=0, tiled=True)  45.4 us
    pallas_call x1, Pallas kernels, shards(): local_call(build_kernel, packed, [SM, SM, VM, VM], [boxes], 'build')  18.5 us
    pallas_call x1, Pallas kernels, shards(): local_call(read_kernel, jax.ShapeDtypeStruct(marker_positions.shape, jnp....  15.8 us
    pallas_call x1, Pallas kernels, shards(): local_call(place_kernel, jax.ShapeDtypeStruct(fluid_source.shape, jnp.flo...  15.4 us
    pallas_call x1, Pallas kernels, shards(): local_call(pick_kernel, packed, [SM, VM], [boxes, grid], 'pick')  14.2 us
    unnamed x8, local copies, waits for them, and re-layouts  5.6 us

profile of v1, /device:TPU:0, one launch (start us, length us, event | category | flops | bytes accessed | tf_op | source)
XLA Modules:
  0.0 217.0 jit_solution(13545990746808396082)
XLA Ops:
  0.6 0.9 convert_reduce_fusion
  1.5 1.2 multiply_add_fusion.1.slot_ref
  2.7 0.8 copy.20
  3.5 0.7 reshape.21.base_ref
  4.2 2.1 copy.22.force_ref
  6.3 2.4 %negate_select_fusion.1 = (f32[128,3,256]{2,1,0:T(4,128)S(1)}, f32[128,3,256]{2,1,0:T(4,128)S(1)}) fusion(f32[128,3,256]{2,0,1:T(8,128)} %param.7, f32[3]{0:T(128)} %constant.40.clone, f32[3]{0:T(128)} %constant.41.clone), kind=kLoop, calls=%fused_computation.2 | loop fusion | flops 3735552 | bytes 1179672 | tf_op jit(solution)/shard_map/jit(_where)/select_n | solution.py:59
  8.7 1.2 negate_select_fusion
  9.9 1.9 pad_maximum_fusion.table_ref
  11.8 18.5 %build.1 = bf16[6144,128]{1,0:T(8,128)(2,1)} custom-call(s32[128]{0:T(128)} %multiply_add_fusion.1.slot_ref, s32[256]{0:T(256)} %reshape.21.base_ref, f32[128,9,256]{2,1,0:T(8,128)} %pad_maximum_fusion.table_ref, f32[128,3,256]{2,1,0:T(4,128)} %copy.22.force_ref), custom_call_target="tpu_custom_call" | custom-call | tf_op jit(solution)/shard_map/build/pallas_call | solution.py:660
  30.3 45.4 %all_to_all.22 = bf16[32,192,128]{2,1,0:T(8,128)(2,1)S(1)} all-to-all(bf16[32,192,128]{2,1,0:T(8,128)(2,1)} %bitcast.10), channel_id=1, replica_groups=mesh['gz'=32] {'gz'}, dimensions={0} | all-to-all | bytes 3145728 | tf_op jit(solution)/shard_map/all_to_all | solution.py:663
  75.7 0.0 copy-start.1
  75.7 0.4 fusion.4
  76.1 0.7 reshape.23.base_ref
  76.9 0.0 copy-done.1
  76.9 15.4 %place.1.source_ref = f32[4,3,128,128]{3,2,1,0:T(8,128)} custom-call(s32[512]{0:T(512)} %reshape.23.base_ref, bf16[6144,128]{1,0:T(8,128)(2,1)} %bitcast.8, f32[4,3,128,128]{3,2,1,0:T(8,128)} %fluid_ref.1), custom_call_target="tpu_custom_call" | custom-call | tf_op jit(solution)/shard_map/place/pallas_call | solution.py:666
  92.2 46.4 %multigrid.1.velocity_ref = f32[4,3,128,128]{3,2,1,0:T(8,128)} custom-call(f32[4,3,128,128]{3,2,1,0:T(8,128)} %place.1.source_ref), custom_call_target="tpu_custom_call" | custom-call | tf_op jit(solution)/shard_map/multigrid/pallas_call | solution.py:633
  138.6 14.2 %pick.1 = bf16[6144,128]{1,0:T(8,128)(2,1)} custom-call(s32[512]{0:T(512)} %reshape.23.base_ref, f32[4,3,128,128]{3,2,1,0:T(8,128)} %multigrid.1.velocity_ref), custom_call_target="tpu_custom_call" | custom-call | tf_op jit(solution)/shard_map/pick/pallas_call | solution.py:674
  152.9 45.6 %all_to_all.23 = bf16[32,192,128]{2,1,0:T(8,128)(2,1)} all-to-all(bf16[32,192,128]{2,1,0:T(8,128)(2,1)} %bitcast.11), channel_id=1, replica_groups=mesh['gz'=32] {'gz'}, dimensions={0} | all-to-all | bytes 3145728 | tf_op jit(solution)/shard_map/all_to_all | solution.py:677
  198.5 0.0 copy-start
  198.5 15.8 %read.1 = f32[128,3,256]{2,1,0:T(4,128)} custom-call(s32[128]{0:T(128)} %multiply_add_fusion.1.slot_ref, f32[128,9,256]{2,1,0:T(8,128)} %pad_maximum_fusion.table_ref, bf16[6144,128]{1,0:T(8,128)(2,1)} %bitcast.9), custom_call_target="tpu_custom_call" | custom-call | tf_op jit(solution)/shard_map/read/pallas_call | solution.py:678
  214.3 1.9 copy.23
  216.1 0.0 copy-done
  216.1 0.9 copy.29
Async XLA Ops:
  75.7 1.1 copy-start.1
  198.5 17.6 %copy-start = (f32[4,3,128,128]{3,2,1,0:T(8,128)S(1)}, f32[4,3,128,128]{3,2,1,0:T(8,128)}, u32[]{:S(2)}) copy-start(f32[4,3,128,128]{3,2,1,0:T(8,128)} %multigrid.1.velocity_ref) | copy-start | bytes 2359300

commit v2 on v1

--- a/solution.py
+++ b/solution.py
@@ -170,6 +170,10 @@
     lax.fori_loop(0, blocks // 4, some, 0)
 
 
+def rows_of(x):
+    return pl.ds(pl.multiple_of(x * ROWS, 8), ROWS)
+
+
 def place_kernel(base_ref, in_ref, fluid_ref, out_ref, box_ref, grid_ref, twin_ref):
     slots, width = box_ref.shape[0], fluid_ref.shape[2]
     unpack_boxes(in_ref, box_ref)
@@ -194,16 +198,18 @@
             even = moved_box(4 * turn + 2 * part)
             odd = moved_box(4 * turn + 2 * part + 1)
             for (x, piece), (other_x, other_piece) in zip(even, odd):
-                grid_ref[x] += piece
-                twin_ref[other_x] += other_piece
+                grid_ref[rows_of(x), :] += piece
+                twin_ref[rows_of(other_x), :] += other_piece
         return carry
 
     lax.fori_loop(0, slots // 4, some, 0)
     for layer in range(CZ):
         for component in range(3):
             row = component * CZ + layer
-            near = grid_ref[:, row, :] + twin_ref[:, row, :]
-            far = grid_ref[:, HALF + row, :] + twin_ref[:, HALF + row, :]
+            near_rows = pl.ds(row, width, stride=ROWS)
+            far_rows = pl.ds(HALF + row, width, stride=ROWS)
+            near = grid_ref[near_rows, :] + twin_ref[near_rows, :]
+            far = grid_ref[far_rows, :] + twin_ref[far_rows, :]
             far = pltpu.roll(far, 8, 0)
             out_ref[layer, component] = fluid_ref[layer, component] + (near + far)
 
@@ -214,8 +220,8 @@
         for component in range(3):
             row = component * CZ + layer
             low = velocity_ref[layer, component].astype(jnp.bfloat16).astype(jnp.float32)
-            grid_ref[:, row, :] = low
-            grid_ref[:, HALF + row, :] = pltpu.roll(low, width - 8, 0)
+            grid_ref[pl.ds(row, width, stride=ROWS), :] = low
+            grid_ref[pl.ds(HALF + row, width, stride=ROWS), :] = pltpu.roll(low, width - 8, 0)
     lane = lax.broadcasted_iota(jnp.int32, (ROWS, 128), 1)
 
     def one(slot):
@@ -224,7 +230,7 @@
         box = jnp.zeros((ROWS, 128), jnp.float32)
         for step in range(8):
             x = (first_x + step) & (width - 1)
-            moved = pltpu.roll(grid_ref[x], (BOX * step - first_y) & (width - 1), 1)
+            moved = pltpu.roll(grid_ref[rows_of(x), :], (BOX * step - first_y) & (width - 1), 1)
             box = jnp.where(lane // BOX == step, moved, box)
         box_ref[slot] = box
 
@@ -380,7 +386,7 @@
                 body(turn, component)
             return carry
 
-        lax.fori_loop(low, high, step, 0)
+        lax.fori_loop(low, high, step, 0, unroll=True)
 
     def keep(z, c):
         b0[z + 3, c] = source_ref[z, c]
@@ -655,7 +661,7 @@
     slot_index = target * capacity + slot_order
     tables = marker_tables(marker_positions)
     boxes = pltpu.VMEM((slots, ROWS, 128), jnp.float32)
-    grid = pltpu.VMEM((width, ROWS, 128), jnp.float32)
+    grid = pltpu.VMEM((width * ROWS, 128), jnp.float32)
     packed = jax.ShapeDtypeStruct((slots * ROWS, 128), jnp.bfloat16)
     box_sent = local_call(build_kernel, packed, [SM, SM, VM, VM], [boxes], "build")(
         slot_index, base_cells.reshape(-1), tables, marker_forces

time: 218 us -> 211 us (0.968)
  Pallas kernels: 110 us -> 104 us
    pallas_call x1, Pallas kernels: 46.4 us -> 41.6 us  [multigrid(): pl.pallas_call(functools.partial(grid_kernel, devices), out_shape=jax.Sha...]
where the time goes in v2:
time: 211 us
  Pallas kernels  104 us (49%)
  blocking collectives  90.8 us (43%)
  other arithmetic  8.01 us (4%)
  local copies, waits for them, and re-layouts  7.02 us (3%)
    all_to_all x1, blocking collectives, shards(): lax.all_to_all(box_sent, 'gz', split_axis=0, concat_axis=0, tiled=True)  45.4 us
    all_to_all x1, blocking collectives, shards(): lax.all_to_all(picked, 'gz', split_axis=0, concat_axis=0, tiled=True)  45.4 us
    pallas_call x1, Pallas kernels, multigrid(): pl.pallas_call(functools.partial(grid_kernel, devices), out_shape=jax.Sha...  41.6 us
    pallas_call x1, Pallas kernels, shards(): local_call(build_kernel, packed, [SM, SM, VM, VM], [boxes], 'build')  18.5 us
    pallas_call x1, Pallas kernels, shards(): local_call(read_kernel, jax.ShapeDtypeStruct(marker_positions.shape, jnp....  15.8 us
    pallas_call x1, Pallas kernels, shards(): local_call(place_kernel, jax.ShapeDtypeStruct(fluid_source.shape, jnp.flo...  14.5 us
    pallas_call x1, Pallas kernels, shards(): local_call(pick_kernel, packed, [SM, VM], [boxes, grid], 'pick')  13.6 us
    unnamed x8, local copies, waits for them, and re-layouts  5.6 us

profile of v2, /device:TPU:0, one launch (start us, length us, event | category | flops | bytes accessed | tf_op | source)
XLA Modules:
  0.0 210.5 jit_solution(9564488938981870956)
XLA Ops:
  0.6 0.9 convert_reduce_fusion
  1.5 1.2 multiply_add_fusion.1.slot_ref
  2.7 0.8 copy.20
  3.5 0.7 reshape.21.base_ref
  4.2 2.1 copy.22.force_ref
  6.3 2.4 %negate_select_fusion.1 = (f32[128,3,256]{2,1,0:T(4,128)S(1)}, f32[128,3,256]{2,1,0:T(4,128)S(1)}) fusion(f32[128,3,256]{2,0,1:T(8,128)} %param.7, f32[3]{0:T(128)} %constant.40.clone, f32[3]{0:T(128)} %constant.41.clone), kind=kLoop, calls=%fused_computation.2 | loop fusion | flops 3735552 | bytes 1179672 | tf_op jit(solution)/shard_map/jit(_where)/select_n | solution.py:59
  8.7 1.2 negate_select_fusion
  9.9 1.9 pad_maximum_fusion.table_ref
  11.8 18.5 %build.1 = bf16[6144,128]{1,0:T(8,128)(2,1)} custom-call(s32[128]{0:T(128)} %multiply_add_fusion.1.slot_ref, s32[256]{0:T(256)} %reshape.21.base_ref, f32[128,9,256]{2,1,0:T(8,128)} %pad_maximum_fusion.table_ref, f32[128,3,256]{2,1,0:T(4,128)} %copy.22.force_ref), custom_call_target="tpu_custom_call" | custom-call | tf_op jit(solution)/shard_map/build/pallas_call | solution.py:666
  30.3 45.4 %all_to_all.22 = bf16[32,192,128]{2,1,0:T(8,128)(2,1)S(1)} all-to-all(bf16[32,192,128]{2,1,0:T(8,128)(2,1)} %bitcast.10), channel_id=1, replica_groups=mesh['gz'=32] {'gz'}, dimensions={0} | all-to-all | bytes 3145728 | tf_op jit(solution)/shard_map/all_to_all | solution.py:669
  75.7 0.0 copy-start.1
  75.7 0.4 fusion.4
  76.1 0.7 reshape.23.base_ref
  76.9 0.0 copy-done.1
  76.9 14.5 %place.1.source_ref = f32[4,3,128,128]{3,2,1,0:T(8,128)} custom-call(s32[512]{0:T(512)} %reshape.23.base_ref, bf16[6144,128]{1,0:T(8,128)(2,1)} %bitcast.8, f32[4,3,128,128]{3,2,1,0:T(8,128)} %fluid_ref.1), custom_call_target="tpu_custom_call" | custom-call | tf_op jit(solution)/shard_map/place/pallas_call | solution.py:672
  91.3 41.6 %multigrid.1.velocity_ref = f32[4,3,128,128]{3,2,1,0:T(8,128)} custom-call(f32[4,3,128,128]{3,2,1,0:T(8,128)} %place.1.source_ref), custom_call_target="tpu_custom_call" | custom-call | tf_op jit(solution)/shard_map/multigrid/pallas_call | solution.py:639
  133.0 13.6 %pick.1 = bf16[6144,128]{1,0:T(8,128)(2,1)} custom-call(s32[512]{0:T(512)} %reshape.23.base_ref, f32[4,3,128,128]{3,2,1,0:T(8,128)} %multigrid.1.velocity_ref), custom_call_target="tpu_custom_call" | custom-call | tf_op jit(solution)/shard_map/pick/pallas_call | solution.py:680
  146.6 45.4 %all_to_all.23 = bf16[32,192,128]{2,1,0:T(8,128)(2,1)} all-to-all(bf16[32,192,128]{2,1,0:T(8,128)(2,1)} %bitcast.11), channel_id=1, replica_groups=mesh['gz'=32] {'gz'}, dimensions={0} | all-to-all | bytes 3145728 | tf_op jit(solution)/shard_map/all_to_all | solution.py:683
  192.0 0.0 copy-start
  192.0 15.8 %read.1 = f32[128,3,256]{2,1,0:T(4,128)} custom-call(s32[128]{0:T(128)} %multiply_add_fusion.1.slot_ref, f32[128,9,256]{2,1,0:T(8,128)} %pad_maximum_fusion.table_ref, bf16[6144,128]{1,0:T(8,128)(2,1)} %bitcast.9), custom_call_target="tpu_custom_call" | custom-call | tf_op jit(solution)/shard_map/read/pallas_call | solution.py:684
  207.8 1.9 copy.23
  209.6 0.0 copy-done
  209.6 0.9 copy.29
Async XLA Ops:
  75.7 1.1 copy-start.1
  192.0 17.6 %copy-start = (f32[4,3,128,128]{3,2,1,0:T(8,128)S(1)}, f32[4,3,128,128]{3,2,1,0:T(8,128)}, u32[]{:S(2)}) copy-start(f32[4,3,128,128]{3,2,1,0:T(8,128)} %multigrid.1.velocity_ref) | copy-start | bytes 2359300
